TPU v7x, 512 devices: a whole 4x8x8 slice. The times are simulated.
512 devices in a mesh: rows: 64 (over x, y, core), vec: 8 (over z).
Axes of the slice: x: 4, y: 8, z: 8, core: 2. Of those that a mesh axis runs over, the one named last changes fastest.
Arguments:
- vectors: float32 [64, 131072], P('vec', 'rows'), may hold values from -6 to 6
- damage: float32 [131072], P('rows')
- diag_blocks: bfloat16 [1024, 128, 128], P('rows')
- upper_blocks: bfloat16 [8192, 128, 128], P('rows'), may hold values from -0.5 to 0.5
- block_rows: int32 [8192], P('rows'), may hold values from 0 to 1023, as said below
- block_cols: int32 [8192], P('rows'), may hold values from 1 to 1023, as said below
- live_slots: int32 [64], P('rows'), may hold values from 64 to 128, as said below
Outputs:
- product: float32 [64, 131072], P('vec', 'rows')
- projected: float32 [64, 64], P('vec')
Inputs may be any that keep to these rules, and one draw needn't show every extreme that they name: `block_rows`: the slots of device d name block rows d * 16 to (d + 1) * 16 - 1; a slot whose column lies on another device names one of the last 6 of these. block_cols[s] is greater than block_rows[s], and block_cols[s] // 16 lies between d and d + 3 for a slot of device d; some slots reach d + 3. A column on device e other than d is one of the first 6 block rows of e. A pair may appear in several slots; their blocks add. `live_slots`: some device has all its slots stored.
All inputs are finite; a program needn't handle non-finite values.
Results may differ from a plain program's by a relative error of at most 0.0029.
Values may be sent and summed in bfloat16 or wider, within the bound.
No kernel may reach another device: no remote copies, remote signals or barrier semaphores. Data moves between devices by JAX's collectives and lax.ppermute only.
A program may use at most 64 MiB of HBM per device.

v0:
```python
import jax
import jax.numpy as jnp
from jax import lax
from jax.sharding import PartitionSpec as P

REACH = 4
RIM = 6
resid_eta = 0.001


def passed_along(array, axis, by):
    devices = lax.axis_size(axis)
    pairs = [(i, i + by) for i in range(devices) if 0 <= i + by < devices]
    return lax.ppermute(array, axis, pairs)


def on_device(vectors, damage, diag_blocks, upper_blocks, block_rows, block_cols, live_slots):
    vec_here, width = vectors.shape
    rb_here = diag_blocks.shape[0]
    block_size = diag_blocks.shape[1]
    slot_count = upper_blocks.shape[0]
    mine = lax.axis_index("rows")
    soft = jnp.sqrt((1.0 - damage) ** 2 + resid_eta)
    scaled = (vectors * soft[None, :]).astype(jnp.bfloat16).reshape(vec_here, rb_here, block_size)
    stored = (jnp.arange(slot_count) < live_slots[0]).astype(jnp.float32)
    local_rows = block_rows - mine * rb_here
    row_pick = (local_rows[:, None] == jnp.arange(rb_here)[None, :]).astype(jnp.float32) * stored[
        :, None
    ]
    own_rows = jnp.einsum(
        "vrb,sr->vsb", scaled, row_pick.astype(jnp.bfloat16), preferred_element_type=jnp.float32
    ).astype(jnp.bfloat16)
    accum = jnp.einsum("vrj,rij->vri", scaled, diag_blocks, preferred_element_type=jnp.float32)
    backward = jnp.einsum(
        "vsi,sij->vsj", own_rows, upper_blocks, preferred_element_type=jnp.float32
    )
    pieces = [scaled]
    for step in range(1, REACH):
        pieces.append(passed_along(scaled[:, :RIM], "rows", -step))
    window = jnp.concatenate(pieces, axis=1)
    relative = block_cols - mine * rb_here
    dev_step = relative // rb_here
    within = relative - dev_step * rb_here
    col_index = jnp.where(dev_step == 0, within, rb_here + (dev_step - 1) * RIM + within)
    span = window.shape[1]
    col_pick = (col_index[:, None] == jnp.arange(span)[None, :]).astype(jnp.float32) * stored[
        :, None
    ]
    far_cols = jnp.einsum(
        "vcb,sc->vsb", window, col_pick.astype(jnp.bfloat16), preferred_element_type=jnp.float32
    ).astype(jnp.bfloat16)
    forward = jnp.einsum("vsj,sij->vsi", far_cols, upper_blocks, preferred_element_type=jnp.float32)
    gathered = jnp.einsum("vsi,sr->vri", forward, row_pick, precision=lax.Precision.HIGHEST)
    spread = jnp.einsum("vsj,sc->vcj", backward, col_pick, precision=lax.Precision.HIGHEST)
    gathered, spread = (gathered, spread)
    accum = accum + gathered + spread[:, :rb_here]
    for step in range(1, REACH):
        low = rb_here + (step - 1) * RIM
        arrived = passed_along(spread[:, low : low + RIM], "rows", step)
        accum = accum.at[:, :RIM].add(arrived)
    product = soft[None, :] * accum.reshape(vec_here, width)
    partial_gram = jnp.dot(
        vectors,
        lax.all_gather(product.astype(jnp.bfloat16), "vec", axis=0, tiled=True)
        .astype(jnp.float32)
        .T,
        precision=lax.Precision.HIGHEST,
        preferred_element_type=jnp.float32,
    )
    total_dof = width * lax.axis_size("rows")
    projected = lax.psum(partial_gram, "rows") / total_dof
    return (product, projected)


def solution(mesh):
    return jax.shard_map(
        on_device,
        mesh=mesh,
        in_specs=(
            P("vec", "rows"),
            P("rows"),
            P("rows", None, None),
            P("rows", None, None),
            P("rows"),
            P("rows"),
            P("rows"),
        ),
        out_specs=(P("vec", "rows"), P("vec", None)),
        check_vma=False,
    )
```

profile of v0, /device:TPU:1, one launch (start us, length us, event | category | flops | bytes accessed | tf_op | source)
XLA Modules:
  0.0 186.2 jit_solution(1229719728883084545)
XLA Ops:
  0.6 0.0 copy-start
  0.6 0.8 add_sqrt_fusion
  1.4 0.9 fusion.16
  2.3 1.3 collective-permute-start.2
  3.6 1.3 collective-permute-start.1
  4.9 8.8 %collective-permute-start = (bf16[8,6,128]{2,0,1:T(8,128)(2,1)S(1)}, bf16[8,6,128]{2,0,1:T(8,128)(2,1)S(1)}, u32[]{:S(2)}, u32[]{:S(2)}) collective-permute-start(bf16[8,6,128]{2,0,1:T(8,128)(2,1)S(1)} %slice.91), channel_id=1, source_target_pairs={{8,0},{16,8},{24,16},{32,24},{40,32},{48,40},{56,48},{64,56},{72,6... | collective-permute-start | bytes 36872 | tf_op jit(solution)/shard_map/ppermute | solution.py:14
  14.3 0.8 broadcast_subtract_fusion
  15.2 0.8 compare_select_fusion
  16.0 0.3 fusion.17
  16.3 3.4 %fusion.12 = f32[128,8,128]{2,1,0:T(8,128)S(1)} fusion(bf16[128,128,128]{2,1,0:T(8,128)(2,1)} %param.16, bf16[128,8,128]{2,0,1:T(8,128)(2,1)S(1)} %fusion.17), kind=kOutput, calls=%fused_computation.15 | convolution fusion | flops 33554432 | bytes 4980736 | tf_op jit(solution)/shard_map/vsi,sij->vsj/dot_general | solution.py:34
  19.7 0.5 fusion.2
  20.1 0.0 copy-start.2
  20.2 6.0 %collective-permute-start.5 = (f32[8,6,128]{2,0,1:T(8,128)S(1)}, f32[8,6,128]{2,0,1:T(8,128)S(1)}, u32[]{:S(2)}, u32[]{:S(2)}) collective-permute-start(f32[8,6,128]{2,0,1:T(8,128)S(1)} %get-tuple-element.40), channel_id=1, source_target_pairs={{0,24},{8,32},{16,40},{24,48},{32,56},{40,64},{48,72},{56,80},{64,... | collective-permute-start | bytes 73736 | tf_op jit(solution)/shard_map/ppermute | solution.py:14
  26.2 3.4 %collective-permute-start.4 = (f32[8,6,128]{2,0,1:T(8,128)S(1)}, f32[8,6,128]{2,0,1:T(8,128)S(1)}, u32[]{:S(2)}, u32[]{:S(2)}) collective-permute-start(f32[8,6,128]{2,0,1:T(8,128)S(1)} %get-tuple-element.41), channel_id=1, source_target_pairs={{0,16},{8,24},{16,32},{24,40},{32,48},{40,56},{48,64},{56,72},{64,... | collective-permute-start | bytes 73736 | tf_op jit(solution)/shard_map/ppermute | solution.py:14
  29.5 1.9 %collective-permute-start.3 = (f32[8,6,128]{2,0,1:T(8,128)S(1)}, f32[8,6,128]{2,0,1:T(8,128)S(1)}, u32[]{:S(2)}, u32[]{:S(2)}) collective-permute-start(f32[8,6,128]{2,0,1:T(8,128)S(1)} %get-tuple-element.42), channel_id=1, source_target_pairs={{0,8},{8,16},{16,24},{24,32},{32,40},{40,48},{48,56},{56,64},{64,7... | collective-permute-start | bytes 73736 | tf_op jit(solution)/shard_map/ppermute | solution.py:14
  31.5 0.3 fusion.14
  31.8 2.3 %fusion.9 = f32[128,8,128]{2,1,0:T(8,128)S(1)} fusion(bf16[128,128,128]{2,1,0:T(8,128)(2,1)S(1)} %copy-done.1, bf16[128,8,128]{2,0,1:T(8,128)(2,1)S(1)} %fusion.14), kind=kOutput, calls=%fused_computation.13 | convolution fusion | flops 33554432 | bytes 4980736 | tf_op jit(solution)/shard_map/vsj,sij->vsi/dot_general | solution.py:52
  34.0 0.4 fusion.4
  34.5 0.4 fusion.1
  34.9 0.6 fusion.39
  35.6 20.4 %all_gather.3 = bf16[64,2048]{1,0:T(8,128)(2,1)S(1)} all-gather(bf16[8,2048]{1,0:T(8,128)(2,1)S(1)} %get-tuple-element.38), channel_id=1, replica_groups=mesh['rows'=64,'vec'=8] {'vec'}, dimensions={0}, use_global_device_ids=true | all-gather | bytes 294912 | tf_op jit(solution)/shard_map/all_gather | solution.py:64
  56.0 0.3 convolution_bitcast_fusion
  56.3 129.3 %psum.7 = f32[8,64]{1,0:T(8,128)S(1)} all-reduce(f32[8,64]{1,0:T(8,128)S(1)} %convolution_bitcast_fusion), channel_id=1, replica_groups=mesh['rows'=64,'vec'=8] {'rows'}, use_global_device_ids=true, to_apply=%region_0.1 | all-reduce | flops 512 | bytes 4096 | tf_op jit(solution)/shard_map/psum | solution.py:71
  185.6 0.6 broadcast_multiply_fusion
  (19 shorter events, 0.1 us)
Async XLA Ops:
  0.6 33.8 %copy-start = (bf16[16,128,128]{2,1,0:T(8,128)(2,1)S(1)}, bf16[16,128,128]{2,1,0:T(8,128)(2,1)}, u32[]{:S(2)}) copy-start(bf16[16,128,128]{2,1,0:T(8,128)(2,1)} %param.15) | copy-start | bytes 1572868
  2.3 27.2 %collective-permute-start.2 = (bf16[8,6,128]{2,0,1:T(8,128)(2,1)S(1)}, bf16[8,6,128]{2,0,1:T(8,128)(2,1)S(1)}, u32[]{:S(2)}, u32[]{:S(2)}) collective-permute-start(bf16[8,6,128]{2,0,1:T(8,128)(2,1)S(1)} %slice.91), channel_id=1, source_target_pairs={{24,0},{32,8},{40,16},{48,24},{56,32},{64,40},{72,48},{80,56},{88,... | collective-permute-start | bytes 36872 | tf_op jit(solution)/shard_map/ppermute | solution.py:14
  3.6 27.9 %collective-permute-start.1 = (bf16[8,6,128]{2,0,1:T(8,128)(2,1)S(1)}, bf16[8,6,128]{2,0,1:T(8,128)(2,1)S(1)}, u32[]{:S(2)}, u32[]{:S(2)}) collective-permute-start(bf16[8,6,128]{2,0,1:T(8,128)(2,1)S(1)} %slice.91), channel_id=1, source_target_pairs={{16,0},{24,8},{32,16},{40,24},{48,32},{56,40},{64,48},{72,56},{80,... | collective-permute-start | bytes 36872 | tf_op jit(solution)/shard_map/ppermute | solution.py:14
  4.9 26.6 %collective-permute-start = (bf16[8,6,128]{2,0,1:T(8,128)(2,1)S(1)}, bf16[8,6,128]{2,0,1:T(8,128)(2,1)S(1)}, u32[]{:S(2)}, u32[]{:S(2)}) collective-permute-start(bf16[8,6,128]{2,0,1:T(8,128)(2,1)S(1)} %slice.91), channel_id=1, source_target_pairs={{8,0},{16,8},{24,16},{32,24},{40,32},{48,40},{56,48},{64,56},{72,6... | collective-permute-start | bytes 36872 | tf_op jit(solution)/shard_map/ppermute | solution.py:14
  14.3 17.4 %copy-start.1 = (bf16[128,128,128]{2,1,0:T(8,128)(2,1)S(1)}, bf16[128,128,128]{2,1,0:T(8,128)(2,1)}, u32[]{:S(2)}) copy-start(bf16[128,128,128]{2,1,0:T(8,128)(2,1)} %param.16) | copy-start | bytes 12582916
  20.1 35.9 %copy-start.2 = (f32[8,2048]{1,0:T(8,128)S(1)}, f32[8,2048]{1,0:T(8,128)}, u32[]{:S(2)}) copy-start(f32[8,2048]{1,0:T(8,128)} %param.13) | copy-start | bytes 196612
  20.2 14.7 %collective-permute-start.5 = (f32[8,6,128]{2,0,1:T(8,128)S(1)}, f32[8,6,128]{2,0,1:T(8,128)S(1)}, u32[]{:S(2)}, u32[]{:S(2)}) collective-permute-start(f32[8,6,128]{2,0,1:T(8,128)S(1)} %get-tuple-element.40), channel_id=1, source_target_pairs={{0,24},{8,32},{16,40},{24,48},{32,56},{40,64},{48,72},{56,80},{64,... | collective-permute-start | bytes 73736 | tf_op jit(solution)/shard_map/ppermute | solution.py:14
  26.2 8.7 %collective-permute-start.4 = (f32[8,6,128]{2,0,1:T(8,128)S(1)}, f32[8,6,128]{2,0,1:T(8,128)S(1)}, u32[]{:S(2)}, u32[]{:S(2)}) collective-permute-start(f32[8,6,128]{2,0,1:T(8,128)S(1)} %get-tuple-element.41), channel_id=1, source_target_pairs={{0,16},{8,24},{16,32},{24,40},{32,48},{40,56},{48,64},{56,72},{64,... | collective-permute-start | bytes 73736 | tf_op jit(solution)/shard_map/ppermute | solution.py:14
  29.5 5.3 %collective-permute-start.3 = (f32[8,6,128]{2,0,1:T(8,128)S(1)}, f32[8,6,128]{2,0,1:T(8,128)S(1)}, u32[]{:S(2)}, u32[]{:S(2)}) collective-permute-start(f32[8,6,128]{2,0,1:T(8,128)S(1)} %get-tuple-element.42), channel_id=1, source_target_pairs={{0,8},{8,16},{16,24},{24,32},{32,40},{40,48},{48,56},{56,64},{64,7... | collective-permute-start | bytes 73736 | tf_op jit(solution)/shard_map/ppermute | solution.py:14
where the time goes:
time: 187 us; the launch traced here: 186 us
  blocking collectives  150 us (80%)
  starting transfers between devices  22.6 us (12%)
  matrix products  7.72 us (4%)
  other arithmetic  4.55 us (2%)
    psum x1, blocking collectives, on_device(): projected = lax.psum(partial_gram, 'rows') / total_dof  129 us
    ppermute x6, starting transfers between devices, passed_along(): return lax.ppermute(array, axis, pairs)  22.6 us
    all_gather x1, blocking collectives, on_device(): lax.all_gather(product.astype(jnp.bfloat16), 'vec', axis=0, tiled=True)  20.4 us
  transfers between devices with their start and end apart: 6, of which 0 were waited for; matrix products, arithmetic and copies ran while one was open for 5% of the time, Pallas kernels for 0%

commit v1 on v0

--- a/solution.py
+++ b/solution.py
@@ -6,6 +6,11 @@
 REACH = 4
 RIM = 6
 resid_eta = 0.001
+
+
+def gather_over(shard, name, dim):
+    outgoing = jnp.stack([shard] * lax.axis_size(name))
+    return jnp.concatenate(lax.all_to_all(outgoing, name, 0, 0), axis=dim)
 
 
 def passed_along(array, axis, by):
@@ -61,9 +66,7 @@
     product = soft[None, :] * accum.reshape(vec_here, width)
     partial_gram = jnp.dot(
         vectors,
-        lax.all_gather(product.astype(jnp.bfloat16), "vec", axis=0, tiled=True)
-        .astype(jnp.float32)
-        .T,
+        gather_over(product.astype(jnp.bfloat16), "vec", 0).astype(jnp.float32).T,
         precision=lax.Precision.HIGHEST,
         preferred_element_type=jnp.float32,
     )

time: 187 us -> 178 us (0.952)
  blocking collectives: 150 us -> 141 us
    all_gather x1 -> x0, blocking collectives: 20.4 us -> none  [on_device(): lax.all_gather(product.astype(jnp.bfloat16), 'vec', axis=0, tiled=True)]
    all_to_all x0 -> x1, blocking collectives: none -> 17.5 us  [gather_over(): return jnp.concatenate(lax.all_to_all(outgoing, name, 0, 0), axis=dim)]
    psum x1, blocking collectives: 129 us -> 124 us  [on_device(): projected = lax.psum(partial_gram, 'rows') / total_dof]
where the time goes in v1:
time: 178 us
  blocking collectives  141 us (79%)
  starting transfers between devices  22.6 us (13%)
  matrix products  7.72 us (4%)
  other arithmetic  4.55 us (3%)
    psum x1, blocking collectives, on_device(): projected = lax.psum(partial_gram, 'rows') / total_dof  124 us
    ppermute x6, starting transfers between devices, passed_along(): return lax.ppermute(array, axis, pairs)  22.6 us
    all_to_all x1, blocking collectives, gather_over(): return jnp.concatenate(lax.all_to_all(outgoing, name, 0, 0), axis=dim)  17.5 us
  transfers between devices with their start and end apart: 6, of which 0 were waited for; matrix products, arithmetic and copies ran while one was open for 5% of the time, Pallas kernels for 0%

profile of v1, /device:TPU:1, one launch (start us, length us, event | category | flops | bytes accessed | tf_op | source)
XLA Modules:
  0.0 177.8 jit_solution(8539367013519874851)
XLA Ops:
  0.6 0.0 copy-start
  0.6 0.8 add_sqrt_fusion
  1.4 0.9 fusion.17
  2.3 1.3 collective-permute-start.2
  3.6 1.3 collective-permute-start.1
  4.9 8.8 %collective-permute-start = (bf16[8,6,128]{2,0,1:T(8,128)(2,1)S(1)}, bf16[8,6,128]{2,0,1:T(8,128)(2,1)S(1)}, u32[]{:S(2)}, u32[]{:S(2)}) collective-permute-start(bf16[8,6,128]{2,0,1:T(8,128)(2,1)S(1)} %slice.91), channel_id=1, source_target_pairs={{8,0},{16,8},{24,16},{32,24},{40,32},{48,40},{56,48},{64,56},{72,6... | collective-permute-start | bytes 36872 | tf_op jit(solution)/shard_map/ppermute | solution.py:19
  14.3 0.8 broadcast_subtract_fusion
  15.2 0.8 compare_select_fusion
  16.0 0.3 fusion.18
  16.3 3.4 %fusion.12 = f32[128,8,128]{2,1,0:T(8,128)S(1)} fusion(bf16[128,128,128]{2,1,0:T(8,128)(2,1)} %param.16, bf16[128,8,128]{2,0,1:T(8,128)(2,1)S(1)} %fusion.18), kind=kOutput, calls=%fused_computation.15 | convolution fusion | flops 33554432 | bytes 4980736 | tf_op jit(solution)/shard_map/vsi,sij->vsj/dot_general | solution.py:39
  19.7 0.5 fusion.2
  20.2 0.0 copy-start.2
  20.2 6.0 %collective-permute-start.5 = (f32[8,6,128]{2,0,1:T(8,128)S(1)}, f32[8,6,128]{2,0,1:T(8,128)S(1)}, u32[]{:S(2)}, u32[]{:S(2)}) collective-permute-start(f32[8,6,128]{2,0,1:T(8,128)S(1)} %get-tuple-element.40), channel_id=1, source_target_pairs={{0,24},{8,32},{16,40},{24,48},{32,56},{40,64},{48,72},{56,80},{64,... | collective-permute-start | bytes 73736 | tf_op jit(solution)/shard_map/ppermute | solution.py:19
  26.2 3.4 %collective-permute-start.4 = (f32[8,6,128]{2,0,1:T(8,128)S(1)}, f32[8,6,128]{2,0,1:T(8,128)S(1)}, u32[]{:S(2)}, u32[]{:S(2)}) collective-permute-start(f32[8,6,128]{2,0,1:T(8,128)S(1)} %get-tuple-element.41), channel_id=1, source_target_pairs={{0,16},{8,24},{16,32},{24,40},{32,48},{40,56},{48,64},{56,72},{64,... | collective-permute-start | bytes 73736 | tf_op jit(solution)/shard_map/ppermute | solution.py:19
  29.5 1.9 %collective-permute-start.3 = (f32[8,6,128]{2,0,1:T(8,128)S(1)}, f32[8,6,128]{2,0,1:T(8,128)S(1)}, u32[]{:S(2)}, u32[]{:S(2)}) collective-permute-start(f32[8,6,128]{2,0,1:T(8,128)S(1)} %get-tuple-element.42), channel_id=1, source_target_pairs={{0,8},{8,16},{16,24},{24,32},{32,40},{40,48},{48,56},{56,64},{64,7... | collective-permute-start | bytes 73736 | tf_op jit(solution)/shard_map/ppermute | solution.py:19
  31.5 0.3 fusion.15
  31.8 2.3 %fusion.9 = f32[128,8,128]{2,1,0:T(8,128)S(1)} fusion(bf16[128,128,128]{2,1,0:T(8,128)(2,1)S(1)} %copy-done.1, bf16[128,8,128]{2,0,1:T(8,128)(2,1)S(1)} %fusion.15), kind=kOutput, calls=%fused_computation.13 | convolution fusion | flops 33554432 | bytes 4980736 | tf_op jit(solution)/shard_map/vsj,sij->vsi/dot_general | solution.py:57
  34.0 0.4 fusion.4
  34.5 0.4 fusion.1
  34.9 0.6 fusion.40
  35.6 17.5 %all_to_all.5 = bf16[8,8,2048]{2,1,0:T(8,128)(2,1)S(1)} all-to-all(bf16[8,8,2048]{2,1,0:T(8,128)(2,1)S(1)} %stack.2), channel_id=1, replica_groups=mesh['rows'=64,'vec'=8] {'vec'}, dimensions={0} | all-to-all | bytes 524288 | tf_op jit(solution)/shard_map/all_to_all | solution.py:13
  53.1 0.3 convolution_bitcast_fusion
  53.4 123.9 %psum.7 = f32[8,64]{1,0:T(8,128)S(1)} all-reduce(f32[8,64]{1,0:T(8,128)S(1)} %convolution_bitcast_fusion), channel_id=1, replica_groups=mesh['rows'=64,'vec'=8] {'rows'}, use_global_device_ids=true, to_apply=%region_0.1 | all-reduce | flops 512 | bytes 4096 | tf_op jit(solution)/shard_map/psum | solution.py:74
  177.2 0.6 broadcast_multiply_fusion
  (20 shorter events, 0.1 us)
Async XLA Ops:
  0.6 33.8 %copy-start = (bf16[16,128,128]{2,1,0:T(8,128)(2,1)S(1)}, bf16[16,128,128]{2,1,0:T(8,128)(2,1)}, u32[]{:S(2)}) copy-start(bf16[16,128,128]{2,1,0:T(8,128)(2,1)} %param.15) | copy-start | bytes 1572868
  2.3 27.2 %collective-permute-start.2 = (bf16[8,6,128]{2,0,1:T(8,128)(2,1)S(1)}, bf16[8,6,128]{2,0,1:T(8,128)(2,1)S(1)}, u32[]{:S(2)}, u32[]{:S(2)}) collective-permute-start(bf16[8,6,128]{2,0,1:T(8,128)(2,1)S(1)} %slice.91), channel_id=1, source_target_pairs={{24,0},{32,8},{40,16},{48,24},{56,32},{64,40},{72,48},{80,56},{88,... | collective-permute-start | bytes 36872 | tf_op jit(solution)/shard_map/ppermute | solution.py:19
  3.6 27.9 %collective-permute-start.1 = (bf16[8,6,128]{2,0,1:T(8,128)(2,1)S(1)}, bf16[8,6,128]{2,0,1:T(8,128)(2,1)S(1)}, u32[]{:S(2)}, u32[]{:S(2)}) collective-permute-start(bf16[8,6,128]{2,0,1:T(8,128)(2,1)S(1)} %slice.91), channel_id=1, source_target_pairs={{16,0},{24,8},{32,16},{40,24},{48,32},{56,40},{64,48},{72,56},{80,... | collective-permute-start | bytes 36872 | tf_op jit(solution)/shard_map/ppermute | solution.py:19
  4.9 26.6 %collective-permute-start = (bf16[8,6,128]{2,0,1:T(8,128)(2,1)S(1)}, bf16[8,6,128]{2,0,1:T(8,128)(2,1)S(1)}, u32[]{:S(2)}, u32[]{:S(2)}) collective-permute-start(bf16[8,6,128]{2,0,1:T(8,128)(2,1)S(1)} %slice.91), channel_id=1, source_target_pairs={{8,0},{16,8},{24,16},{32,24},{40,32},{48,40},{56,48},{64,56},{72,6... | collective-permute-start | bytes 36872 | tf_op jit(solution)/shard_map/ppermute | solution.py:19
  14.3 17.4 %copy-start.1 = (bf16[128,128,128]{2,1,0:T(8,128)(2,1)S(1)}, bf16[128,128,128]{2,1,0:T(8,128)(2,1)}, u32[]{:S(2)}) copy-start(bf16[128,128,128]{2,1,0:T(8,128)(2,1)} %param.16) | copy-start | bytes 12582916
  20.2 32.9 %copy-start.2 = (f32[8,2048]{1,0:T(8,128)S(1)}, f32[8,2048]{1,0:T(8,128)}, u32[]{:S(2)}) copy-start(f32[8,2048]{1,0:T(8,128)} %param.13) | copy-start | bytes 196612
  20.2 14.7 %collective-permute-start.5 = (f32[8,6,128]{2,0,1:T(8,128)S(1)}, f32[8,6,128]{2,0,1:T(8,128)S(1)}, u32[]{:S(2)}, u32[]{:S(2)}) collective-permute-start(f32[8,6,128]{2,0,1:T(8,128)S(1)} %get-tuple-element.40), channel_id=1, source_target_pairs={{0,24},{8,32},{16,40},{24,48},{32,56},{40,64},{48,72},{56,80},{64,... | collective-permute-start | bytes 73736 | tf_op jit(solution)/shard_map/ppermute | solution.py:19
  26.2 8.7 %collective-permute-start.4 = (f32[8,6,128]{2,0,1:T(8,128)S(1)}, f32[8,6,128]{2,0,1:T(8,128)S(1)}, u32[]{:S(2)}, u32[]{:S(2)}) collective-permute-start(f32[8,6,128]{2,0,1:T(8,128)S(1)} %get-tuple-element.41), channel_id=1, source_target_pairs={{0,16},{8,24},{16,32},{24,40},{32,48},{40,56},{48,64},{56,72},{64,... | collective-permute-start | bytes 73736 | tf_op jit(solution)/shard_map/ppermute | solution.py:19
  29.5 5.3 %collective-permute-start.3 = (f32[8,6,128]{2,0,1:T(8,128)S(1)}, f32[8,6,128]{2,0,1:T(8,128)S(1)}, u32[]{:S(2)}, u32[]{:S(2)}) collective-permute-start(f32[8,6,128]{2,0,1:T(8,128)S(1)} %get-tuple-element.42), channel_id=1, source_target_pairs={{0,8},{8,16},{16,24},{24,32},{32,40},{40,48},{48,56},{56,64},{64,7... | collective-permute-start | bytes 73736 | tf_op jit(solution)/shard_map/ppermute | solution.py:19
